TPU v7x, 512 devices: a whole 4x4x16 slice. The times are simulated.
512 devices in a mesh: ctx: 64 (over x, z), head: 8 (over y, core).
Axes of the slice: x: 4, y: 4, z: 16, core: 2. Of those that a mesh axis runs over, the one named last changes fastest.
Arguments:
- prefix_len: int32 [2], replicated, may hold values from 2048 to 16384, as said below
- page_slot: int32 [2, 64], replicated, may hold values from 0 to 127, as said below
- queries: bfloat16 [512, 8192], P('ctx', 'head'), may hold values from -6 to 6
- new_kv: bfloat16 [2, 512, 1024], P(None, 'ctx', 'head'), may hold values from -6 to 6
- cache: bfloat16 [2, 128, 256, 1024], P(None, 'ctx', None, 'head'), may hold values from -6 to 6
Outputs:
- attention: bfloat16 [512, 8192], P(('ctx', 'head'))
Inputs may be any that keep to these rules, and one draw needn't show every extreme that they name: `prefix_len`: each conversation's prefix holds 2048 to 16384 tokens; one conversation holds exactly 16384. `page_slot`: every slot number appears once; slot s lies at ctx index s // 2, as its slot s % 2.
All inputs are finite; a program needn't handle non-finite values.
Results may differ from a plain program's by a relative error of at most 0.0075.
Values may be sent and summed in bfloat16 or wider, within the bound.
A program may use at most 64 MiB of HBM per device.

v0:
```python
import jax
import jax.numpy as jnp
from jax import lax
from jax.sharding import PartitionSpec as P

HEAD_DIM = 128
SPAN = 256
PAGE = 256
MAXPAGES = 64


MASKED = -1e30


def slot_owners(page_slot, first_slot, slot_count):
    flat_table = page_slot.reshape(-1)
    wanted = first_slot + jnp.arange(slot_count, dtype=jnp.int32)
    matches = (flat_table[None, :] == wanted[:, None]).astype(jnp.int32)
    item_ids = jnp.arange(flat_table.shape[0], dtype=jnp.int32)
    return jnp.sum(matches * item_ids[None, :], axis=1)


def raise_rows(row_max, row_start, candidate):
    previous = lax.dynamic_slice_in_dim(row_max, row_start, candidate.shape[0], 0)
    return lax.dynamic_update_slice_in_dim(row_max, jnp.maximum(previous, candidate), row_start, 0)


def add_rows(totals, row_start, term):
    previous = lax.dynamic_slice_in_dim(totals, row_start, term.shape[0], 0)
    return lax.dynamic_update_slice_in_dim(totals, previous + term, row_start, 0)


def weigh_scores(scores, row_top):
    return jnp.exp(scores - row_top[..., None]).astype(jnp.bfloat16)


def local(prefix_len, page_slot, queries, new_kv, cache):
    own_rows = queries.shape[0]
    kv_local = new_kv.shape[2] // HEAD_DIM
    group_size = queries.shape[1] // HEAD_DIM // kv_local
    slot_count = cache.shape[1]
    score_scale = HEAD_DIM ** (-0.5)
    ctx_place = lax.axis_index("ctx")
    gathered = lax.all_gather(queries, "ctx", axis=0, tiled=True)
    total_rows = gathered.shape[0]
    gathered = gathered.reshape(total_rows, kv_local, group_size, HEAD_DIM)
    slot_items = slot_owners(page_slot, ctx_place * slot_count, slot_count)
    slot_dialog = slot_items // MAXPAGES
    slot_page = slot_items % MAXPAGES
    dialog_ids = jnp.arange(prefix_len.shape[0], dtype=jnp.int32)
    slot_length = jnp.sum(
        (dialog_ids[None, :] == slot_dialog[:, None]).astype(jnp.int32) * prefix_len[None, :],
        axis=1,
    )
    key_pages = cache[0].reshape(slot_count, PAGE, kv_local, HEAD_DIM)
    value_pages = cache[1].reshape(slot_count, PAGE, kv_local, HEAD_DIM)
    offsets = jnp.arange(PAGE, dtype=jnp.int32)

    def slot_start(slot_index):
        return slot_dialog[slot_index] * SPAN

    def slot_scores(slot_index):
        query_rows = lax.dynamic_slice_in_dim(gathered, slot_start(slot_index), SPAN, 0)
        page_keys = lax.dynamic_index_in_dim(key_pages, slot_index, 0, keepdims=False)
        raw_scores = (
            jnp.einsum("tghd,pgd->tghp", query_rows, page_keys, preferred_element_type=jnp.float32)
            * score_scale
        )
        live_keys = slot_page[slot_index] * PAGE + offsets < slot_length[slot_index]
        return jnp.where(live_keys, raw_scores, MASKED)

    def max_step(slot_index, row_max):
        return raise_rows(row_max, slot_start(slot_index), jnp.max(slot_scores(slot_index), axis=3))

    row_max = jnp.full((total_rows, kv_local, group_size), MASKED, jnp.float32)
    row_max = lax.fori_loop(0, slot_count, max_step, row_max)
    own_start = ctx_place * own_rows
    own_dialog_start = own_start // SPAN * SPAN
    own_offset = own_start % SPAN
    turn_steps = jnp.arange(SPAN, dtype=jnp.int32)
    own_steps = own_offset + jnp.arange(own_rows, dtype=jnp.int32)
    own_kv = new_kv.reshape(2, own_rows, kv_local, HEAD_DIM)
    dialog_queries = lax.dynamic_slice_in_dim(gathered, own_dialog_start, SPAN, 0)
    self_raw = (
        jnp.einsum("tghd,pgd->tghp", dialog_queries, own_kv[0], preferred_element_type=jnp.float32)
        * score_scale
    )
    causal = own_steps[None, :] <= turn_steps[:, None]
    self_scores = jnp.where(causal[:, None, None, :], self_raw, MASKED)
    self_values = own_kv[1]
    row_max = raise_rows(row_max, own_dialog_start, jnp.max(self_scores, axis=3))
    row_max = lax.pmax(row_max, "ctx")

    def slot_weights(slot_index):
        row_top = lax.dynamic_slice_in_dim(row_max, slot_start(slot_index), SPAN, 0)
        return weigh_scores(slot_scores(slot_index), row_top)

    def slot_values(slot_index, weights):
        page_values = lax.dynamic_index_in_dim(value_pages, slot_index, 0, keepdims=False)
        return jnp.einsum(
            "tghp,pgd->tghd", weights, page_values, preferred_element_type=jnp.float32
        )

    self_top = lax.dynamic_slice_in_dim(row_max, own_dialog_start, self_scores.shape[0], 0)
    self_weights = weigh_scores(self_scores, self_top)
    self_term = jnp.einsum(
        "tghp,pgd->tghd", self_weights, self_values, preferred_element_type=jnp.float32
    )
    self_sum = jnp.sum(self_weights.astype(jnp.float32), axis=3)
    weight_sums = jnp.zeros((total_rows, kv_local, group_size), jnp.float32)

    def sum_step(slot_index, carried):
        value_sums, weight_sums = carried
        row_start = slot_start(slot_index)
        weights = slot_weights(slot_index)
        return (
            add_rows(value_sums, row_start, slot_values(slot_index, weights)),
            add_rows(weight_sums, row_start, jnp.sum(weights.astype(jnp.float32), axis=3)),
        )

    value_sums = jnp.zeros((total_rows, kv_local, group_size, HEAD_DIM), jnp.float32)
    value_sums, weight_sums = lax.fori_loop(0, slot_count, sum_step, (value_sums, weight_sums))
    value_sums = add_rows(value_sums, own_dialog_start, self_term)
    own_sums = lax.psum_scatter(value_sums, "ctx", scatter_dimension=0, tiled=True)
    weight_sums = add_rows(weight_sums, own_dialog_start, self_sum)
    all_weights = lax.psum(weight_sums, "ctx")
    own_weights = lax.dynamic_slice_in_dim(all_weights, own_start, own_rows, 0)
    attention = (own_sums / own_weights[..., None]).astype(jnp.bfloat16)
    attention = attention.reshape(own_rows, kv_local * group_size * HEAD_DIM)
    return lax.all_to_all(attention, "head", split_axis=0, concat_axis=1, tiled=True)


def solution(mesh):
    return jax.shard_map(
        local,
        mesh=mesh,
        in_specs=(P(), P(), P("ctx", "head"), P(None, "ctx", "head"), P(None, "ctx", None, "head")),
        out_specs=P(("ctx", "head"), None),
        check_vma=False,
    )
```

profile of v0, /device:TPU:1, one launch (start us, length us, event | category | flops | bytes accessed | tf_op | source)
XLA Modules:
  0.0 1162.4 jit_solution(1225460248893137209)
XLA Ops:
  6.5 0.7 all-gather.2.cloned.1.call-update
  7.3 0.8 eq.32
  8.1 1.0 slice_bitcast_fusion
  9.4 0.8 fusion.41
  10.3 134.7 %all-gather.2.cloned.1.call-done = bf16[512,1024]{1,0:T(8,128)(2,1)} async-done(((bf16[8,1024]{1,0:T(8,128)(2,1)}), bf16[512,1024]{1,0:T(8,128)(2,1)}) %all-gather.2.cloned.1.call-update) | async-done | bytes 1048592 | tf_op jit(solution)/shard_map/all_gather | solution.py:44
  145.1 1.5 copy.40
  147.3 8.8 while.30
  147.3 0.7 dynamic_slice.205
  149.8 0.7 dynamic_slice.206
  150.5 0.7 fusion.55
  151.6 0.7 dynamic_slice.205
  154.2 0.7 dynamic_slice.206
  154.8 0.7 fusion.55
  156.3 222.5 %pmax.7 = f32[512,1,8]{0,2,1:T(8,128)S(1)} all-reduce(f32[512,1,8]{0,2,1:T(8,128)S(1)} %fusion.34), channel_id=1, replica_groups=mesh['ctx'=64,'head'=8] {'ctx'}, use_global_device_ids=true, to_apply=%region_6.7 | all-reduce | flops 4096 | bytes 32768 | tf_op jit(solution)/shard_map/pmax | solution.py:92
  379.1 10.0 while.31
  379.1 0.7 dynamic_slice.214
  381.6 0.7 dynamic_slice.215
  382.3 0.7 fusion.60
  384.0 0.7 dynamic_slice.214
  386.6 0.7 dynamic_slice.215
  387.2 0.7 fusion.60
  387.9 0.7 convert_reduce_fusion.3
  389.0 1.8 copy.44
  390.8 1.9 copy.45
  392.7 1.7 fusion.28
  394.6 0.7 copy_dynamic-update-slice_fusion
  395.3 1.3 copy-done.1
  397.0 218.9 %psum.7 = f32[512,1,8]{2,0,1:T(8,128)S(1)} all-reduce(f32[512,1,8]{2,0,1:T(8,128)S(1)} %constant_dynamic-update-slice_fusion), channel_id=1, replica_groups=mesh['ctx'=64,'head'=8] {'ctx'}, use_global_device_ids=true, to_apply=%region_12.13 | all-reduce | flops 4096 | bytes 32768 | tf_op jit(solution)/shard_map/psum | solution.py:126
  615.9 516.2 %reduce-scatter.2.cloned.1.call-done = f32[8,1,8,128]{3,2,1,0:T(8,128)} async-done(((f32[512,1,8,128]{3,2,1,0:T(8,128)}), f32[8,1,8,128]{3,2,1,0:T(8,128)}) %reduce-scatter.2.cloned.1.call-update) | async-done | bytes 32784 | tf_op jit(solution)/shard_map/reduce_scatter | solution.py:124
  1132.1 0.8 divide_convert_fusion
  1133.5 0.7 reduce.9
  1134.3 20.7 %all_to_all.17 = bf16[8,2,512]{2,1,0:T(2,128)(2,1)S(1)} all-to-all(bf16[8,2,512]{2,1,0:T(2,128)(2,1)S(1)} %reshape.169), channel_id=1, replica_groups=mesh['ctx'=64,'head'=8] {'head'}, dimensions={0} | all-to-all | bytes 32768 | tf_op jit(solution)/shard_map/all_to_all | solution.py:130
  (46 shorter events, 7.9 us)
Async XLA Ops:
  6.5 138.5 %all-gather.2.cloned.1.call-start = ((), (), s32[]{:S(2)}) async-start(), calls=%async_computation.2 | async-start | bytes 1064960 | tf_op jit(solution)/shard_map/all_gather | solution.py:44
  7.3 1124.9 %reduce-scatter.2.cloned.1.call-start = ((), (), s32[]{:S(2)}) async-start(), calls=%async_computation.3 | async-start | bytes 2129920 | tf_op jit(solution)/shard_map/reduce_scatter | solution.py:124
  147.2 8.8 copy-start.2
  392.7 1.9 copy-start
  395.3 1.4 copy-start.1
Sparse Core Ops, SparseCore 0:
  10.3 134.7 all-gather.1
  396.8 735.2 reduce-scatter.1
where the time goes:
time: 1160 us
  waiting for transfers between devices  652 us (56%)
  blocking collectives  462 us (40%)
  local copies, waits for them, and re-layouts  19.3 us (2%)
  between operations  13.6 us (1%)
    reduce_scatter x1, waiting for transfers between devices, local(): lax.psum_scatter(value_sums, 'ctx', scatter_dimension=0, tiled=True)  516 us
    pmax x1, blocking collectives, local(): row_max = lax.pmax(row_max, 'ctx')  223 us
    psum x1, blocking collectives, local(): all_weights = lax.psum(weight_sums, 'ctx')  219 us
    all_gather x1, waiting for transfers between devices, local(): gathered = lax.all_gather(queries, 'ctx', axis=0, tiled=True)  135 us
  transfers between devices with their start and end apart: 2, of which 2 were waited for; matrix products, arithmetic and copies ran while one was open for 0% of the time, Pallas kernels for 0%

commit v1 on v0

v1 whole, which is shorter than its diff:
```python
import functools

import jax
import jax.numpy as jnp
from jax import lax
from jax.experimental import pallas as pl
from jax.experimental.pallas import tpu as pltpu
from jax.sharding import PartitionSpec as P

HEAD_DIM = 128
PAGE = 256
SLOTS = 2
XS = 4
MASKED = -1e30
FLOOR = -1e20
LOG2E = 1.4426950408889634
MESH = pl.DeviceIdType.MESH
F32 = jnp.float32
BF16 = jnp.bfloat16


def exchange(copies):
    for copy in copies:
        copy.start()
    return copies


def kernel(
    zs, hs, rows, group, lens_ref, slot_ref, q_ref, new_ref, cache_ref, out_ref,
    kv_all, new_all, q_all, part, part_stat, got, got_stat, bias, fin, heads,
    kv_send, kv_recv, new_send, new_recv, q_send, q_recv,
    part_send, part_recv, stat_send, stat_recv, head_send, head_recv, own_sem,
):
    ctx = lax.axis_index("ctx")
    head = lax.axis_index("head")
    x, z = ctx // zs, ctx % zs
    side = x // (XS // 2)
    block = rows * group
    per = rows // hs * group

    def at_x(k):
        return (lax.rem(x + k, XS) * zs + z, head)

    def at_z(there):
        return (x * zs + there, head)

    own_kv = pltpu.make_async_copy(cache_ref, kv_all.at[x], own_sem)
    own_kv.start()

    barrier = pltpu.get_barrier_semaphore()
    for k in range(1, XS):
        pl.semaphore_signal(barrier, inc=1, device_id=at_x(k), device_id_type=MESH)
    for k in range(1, zs):
        pl.semaphore_signal(barrier, inc=1, device_id=at_z(lax.rem(z + k, zs)), device_id_type=MESH)
    for k in range(1, hs):
        pl.semaphore_signal(
            barrier, inc=1, device_id=(ctx, lax.rem(head + k, hs)), device_id_type=MESH
        )

    queries = q_ref[...].astype(F32)
    queries = jnp.concatenate(
        [queries[:, h * HEAD_DIM:(h + 1) * HEAD_DIM] for h in range(group)], axis=0
    )
    q_all[z] = queries.astype(BF16)
    new_all[x] = new_ref[...]

    pl.semaphore_wait(barrier, XS - 1 + zs - 1 + hs - 1)

    kv_copies = exchange([
        pltpu.make_async_remote_copy(
            cache_ref, kv_all.at[x], kv_send.at[k], kv_recv.at[x],
            device_id=at_x(k), device_id_type=MESH,
        )
        for k in (2, 1, 3)
    ])
    q_copies = exchange([
        pltpu.make_async_remote_copy(
            q_all.at[z], q_all.at[z], q_send.at[k], q_recv.at[z],
            device_id=at_z(lax.rem(z + k, zs)), device_id_type=MESH,
        )
        for k in sorted(range(1, zs), key=lambda k: -min(k, zs - k))
    ])
    new_copies = exchange([
        pltpu.make_async_remote_copy(
            new_ref, new_all.at[x], new_send.at[k], new_recv.at[x],
            device_id=at_x(k), device_id_type=MESH,
        )
        for k in (2, 1, 3)
    ])

    pages = slot_ref.shape[1]
    table = slot_ref[pl.ds(side, 1), :]
    page_ids = lax.broadcasted_iota(jnp.int32, (1, pages), 1)
    live = jnp.clip(lens_ref[side] - page_ids * PAGE, 0, PAGE).astype(F32)
    slots = lax.broadcasted_iota(jnp.int32, (XS * SLOTS, pages), 0)
    slots = SLOTS * (slots // SLOTS * zs + z) + slots % SLOTS
    live = jnp.sum(jnp.where(table == slots, live, 0.0), axis=1, keepdims=True)
    offsets = lax.broadcasted_iota(jnp.int32, (XS * SLOTS, PAGE), 1).astype(F32)
    bias[...] = jnp.where(offsets < live, 0.0, MASKED)

    own_kv.wait()

    def wait_from(dst, send, recv, index):
        pltpu.make_async_remote_copy(
            dst.at[index], dst.at[index], send, recv.at[index],
            device_id=(ctx, head), device_id_type=MESH,
        ).wait_recv()

    for k in range(1, zs):
        wait_from(q_all, q_send.at[k], q_recv, lax.rem(z + k, zs))
    for k in range(1, XS):
        wait_from(new_all, new_send.at[k], new_recv, lax.rem(x + k, XS))
        wait_from(kv_all, kv_send.at[k], kv_recv, lax.rem(x + k, XS))

    new_keys = jnp.concatenate([new_all[i, 0].astype(F32) for i in range(XS)], axis=0).astype(BF16)
    new_values = jnp.concatenate([new_all[i, 1].astype(F32) for i in range(XS)], axis=0).astype(BF16)
    fresh = XS * rows
    new_at = lax.broadcasted_iota(jnp.int32, (2 * block, fresh), 1)
    new_rows = rows * (new_at // rows * zs + z) + new_at % rows
    at = lax.broadcasted_iota(jnp.int32, (2 * block, fresh), 0)
    scale = HEAD_DIM ** (-0.5) * LOG2E
    contract = (((1,), (1,)), ((), ()))
    ones = jnp.ones((SLOTS * PAGE, HEAD_DIM), BF16)
    diagonal = (
        lax.broadcasted_iota(jnp.int32, (block, HEAD_DIM), 0)
        == lax.broadcasted_iota(jnp.int32, (block, HEAD_DIM), 1)
    )

    def part_copy(there):
        return pltpu.make_async_remote_copy(
            part.at[there], got.at[z], part_send.at[there], part_recv.at[z],
            device_id=at_z(there), device_id_type=MESH,
        )

    def stat_copy(there):
        return pltpu.make_async_remote_copy(
            part_stat.at[there], got_stat.at[z], stat_send.at[there], stat_recv.at[z],
            device_id=at_z(there), device_id_type=MESH,
        )

    def pair_step(step, carry):
        pair = lax.rem(z // 2 + zs // 4 + step, zs // 2)
        first = pair * 2
        mine = q_all[pl.ds(first, 2)].reshape(2 * block, HEAD_DIM)
        scores = []
        for i in range(XS):
            keys = kv_all[i, 0].reshape(SLOTS * PAGE, HEAD_DIM)
            raw = lax.dot_general(mine, keys, contract, preferred_element_type=F32)
            masks = jnp.concatenate(
                [bias[SLOTS * i + j:SLOTS * i + j + 1, :] for j in range(SLOTS)], axis=1
            )
            scores.append(raw * scale + masks)
        raw = lax.dot_general(mine, new_keys, contract, preferred_element_type=F32)
        q_rows = rows * (x * zs + first + at // block) + at % rows
        seen = (new_rows <= q_rows) & (new_rows >= side * (XS // 2 * zs * rows))
        scores.append(jnp.where(seen, raw * scale, MASKED))
        tops = [jnp.max(s, axis=1, keepdims=True) for s in scores]
        top = functools.reduce(jnp.maximum, tops, jnp.full((2 * block, 1), FLOOR, F32))
        total = jnp.zeros((2 * block, 2 * HEAD_DIM), F32)
        for i in range(XS):
            weights = jnp.exp2(scores[i] - top).astype(BF16)
            values = kv_all[i, 1].reshape(SLOTS * PAGE, HEAD_DIM)
            total += jnp.dot(
                weights, jnp.concatenate([values, ones], axis=1), preferred_element_type=F32
            )
        weights = jnp.exp2(scores[XS] - top).astype(BF16)
        total += jnp.dot(
            weights, jnp.concatenate([new_values, ones[:fresh]], axis=1), preferred_element_type=F32
        )
        amount = total[:, HEAD_DIM:]
        full = jnp.maximum(amount, 1.0)
        normal = (total[:, :HEAD_DIM] / full).astype(BF16)
        stat = jnp.where(amount > 0.0, top + jnp.log2(full), MASKED)
        for j in range(2):
            part[first + j] = normal[j * block:(j + 1) * block]
            part_stat[first + j] = jnp.sum(
                jnp.where(diagonal, stat[j * block:(j + 1) * block], 0.0), axis=0, keepdims=True
            )
        for j in range(2):
            @pl.when(first + j != z)
            def _():
                part_copy(first + j).start()
                stat_copy(first + j).start()
        return carry

    lax.fori_loop(0, zs // 2, pair_step, 0)
    got[z] = part[z]
    got_stat[z] = part_stat[z]
    for k in range(1, zs):
        there = lax.rem(z + k, zs)
        wait_from(got_stat, stat_send.at[there], stat_recv, there)
        wait_from(got, part_send.at[there], part_recv, there)

    stats = [got_stat[i] for i in range(zs)]
    top = functools.reduce(jnp.maximum, stats)
    shares = [jnp.exp2(s - top) for s in stats]
    share_sum = functools.reduce(jnp.add, shares)
    merged = jnp.zeros((block, HEAD_DIM), F32)
    for i in range(zs):
        share = jnp.broadcast_to(shares[i] / share_sum, (block, HEAD_DIM))
        share = jnp.sum(jnp.where(diagonal, share, 0.0), axis=1, keepdims=True)
        merged += share * got[i].astype(F32)
    for h in range(group):
        fin[pl.ds(h, rows, stride=group), :] = merged[h * rows:(h + 1) * rows]

    def fin_at(there):
        return fin.at[pl.ds(pl.multiple_of(there * per, 8), per), :]

    head_copies = exchange([
        pltpu.make_async_remote_copy(
            fin_at(lax.rem(head + k, hs)), heads.at[head], head_send.at[k], head_recv.at[head],
            device_id=(ctx, lax.rem(head + k, hs)), device_id_type=MESH,
        )
        for k in range(1, hs)
    ])
    heads[head] = fin[pl.ds(pl.multiple_of(head * per, 8), per), :]
    for k in range(1, hs):
        wait_from(heads, head_send.at[k], head_recv, lax.rem(head + k, hs))
    out_ref[...] = heads[...]
    for copy in kv_copies + q_copies + new_copies + head_copies:
        copy.wait_send()
    for k in range(1, zs):
        there = lax.rem(z + k, zs)
        part_copy(there).wait_send()
        stat_copy(there).wait_send()


def local(zs, hs, prefix_len, page_slot, queries, new_kv, cache):
    rows = queries.shape[0]
    group = queries.shape[1] // HEAD_DIM
    block = rows * group
    per = rows // hs * group
    dma = pltpu.SemaphoreType.DMA
    result = pl.pallas_call(
        functools.partial(kernel, zs, hs, rows, group),
        out_shape=jax.ShapeDtypeStruct((hs, per, HEAD_DIM), F32),
        in_specs=[
            pl.BlockSpec(memory_space=pltpu.SMEM),
            pl.BlockSpec(memory_space=pltpu.VMEM),
            pl.BlockSpec(memory_space=pltpu.VMEM),
            pl.BlockSpec(memory_space=pltpu.VMEM),
            pl.BlockSpec(memory_space=pl.ANY),
        ],
        out_specs=pl.BlockSpec(memory_space=pltpu.VMEM),
        scratch_shapes=[
            pltpu.VMEM((XS, 2, SLOTS, PAGE, HEAD_DIM), BF16),
            pltpu.VMEM((XS, 2, rows, HEAD_DIM), BF16),
            pltpu.VMEM((zs, block, HEAD_DIM), BF16),
            pltpu.VMEM((zs, block, HEAD_DIM), BF16),
            pltpu.VMEM((zs, 1, HEAD_DIM), F32),
            pltpu.VMEM((zs, block, HEAD_DIM), BF16),
            pltpu.VMEM((zs, 1, HEAD_DIM), F32),
            pltpu.VMEM((XS * SLOTS, PAGE), F32),
            pltpu.VMEM((block, HEAD_DIM), F32),
            pltpu.VMEM((hs, per, HEAD_DIM), F32),
            dma((XS,)), dma((XS,)), dma((XS,)), dma((XS,)), dma((zs,)), dma((zs,)),
            dma((zs,)), dma((zs,)), dma((zs,)), dma((zs,)), dma((hs,)), dma((hs,)), dma,
        ],
        compiler_params=pltpu.CompilerParams(
            collective_id=0, has_side_effects=True, vmem_limit_bytes=48 * 2**20
        ),
    )(prefix_len, page_slot, queries, new_kv, cache.reshape(2, SLOTS, PAGE, HEAD_DIM))
    result = result.reshape(hs, rows // hs, group * HEAD_DIM)
    return result.transpose(1, 0, 2).reshape(rows // hs, hs * group * HEAD_DIM).astype(BF16)


def solution(mesh):
    zs = mesh.shape["ctx"] // XS
    hs = mesh.shape["head"]
    return jax.shard_map(
        functools.partial(local, zs, hs),
        mesh=mesh,
        in_specs=(P(), P(), P("ctx", "head"), P(None, "ctx", "head"), P(None, "ctx", None, "head")),
        out_specs=P(("ctx", "head"), None),
        check_vma=False,
    )
```

time: 1160 us -> 58.1 us (0.05)
  waiting for transfers between devices: 652 us -> 0 us
  blocking collectives: 462 us -> 0 us
  Pallas kernels: 0 us -> 53.5 us
  local copies, waits for them, and re-layouts: 19.3 us -> 4.31 us
  between operations: 13.6 us -> 0.02 us
    reduce_scatter x1 -> x0, waiting for transfers between devices: 516 us -> none  [local(): lax.psum_scatter(value_sums, 'ctx', scatter_dimension=0, tiled=True)]
    pmax x1 -> x0, blocking collectives: 223 us -> none  [local(): row_max = lax.pmax(row_max, 'ctx')]
    psum x1 -> x0, blocking collectives: 219 us -> none  [local(): all_weights = lax.psum(weight_sums, 'ctx')]
    all_gather x1 -> x0, waiting for transfers between devices: 135 us -> none  [local(): gathered = lax.all_gather(queries, 'ctx', axis=0, tiled=True)]
    pallas_call x0 -> x1, Pallas kernels: none -> 53.5 us  [local(): pl.pallas_call(functools.partial(kernel, zs, hs, rows, group), out_shape=...]
    all_to_all x1 -> x0, blocking collectives: 20.7 us -> none  [local(): lax.all_to_all(attention, 'head', split_axis=0, concat_axis=1, tiled=True)]
  transfers between devices with their start and end apart: 2 -> 0, of which waited for: 2 -> 0; matrix products, arithmetic and copies ran while one was open for 0% -> 0% of each run, Pallas kernels for 0% -> 0%
where the time goes in v1:
time: 58.1 us; the launch traced here: 57.8 us
  Pallas kernels  53.5 us (92%)
  local copies, waits for them, and re-layouts  4.31 us (7%)
    pallas_call x1, Pallas kernels, local(): pl.pallas_call(functools.partial(kernel, zs, hs, rows, group), out_shape=...  53.5 us
    unnamed x10, local copies, waits for them, and re-layouts  3.69 us

profile of v1, /device:TPU:1, one launch (start us, length us, event | category | flops | bytes accessed | tf_op | source)
XLA Modules:
  0.0 57.8 jit_solution(11868196342760828033)
XLA Ops:
  0.0 0.0 copy-start
  0.0 0.9 %copy-done = bf16[2,2,256,128]{3,2,1,0:T(8,128)(2,1)S(1)} copy-done((bf16[2,2,256,128]{3,2,1,0:T(8,128)(2,1)S(1)}, bf16[2,2,256,128]{3,2,1,0:T(8,128)(2,1)}, u32[]{:S(2)}) %copy-start) | copy-done | bytes 262168
  1.0 0.0 copy-start.1
  1.0 0.7 %copy-done.1 = bf16[8,1024]{1,0:T(8,128)(2,1)S(1)} copy-done((bf16[8,1024]{1,0:T(8,128)(2,1)S(1)}, bf16[8,1024]{1,0:T(8,128)(2,1)}, u32[]{:S(2)}) %copy-start.1) | copy-done | bytes 16408
  1.7 0.0 copy-start.2
  1.7 0.7 %copy-done.2 = bf16[2,8,128]{2,1,0:T(8,128)(2,1)S(1)} copy-done((bf16[2,8,128]{2,1,0:T(8,128)(2,1)S(1)}, bf16[2,8,128]{2,1,0:T(8,128)(2,1)}, u32[]{:S(2)}) %copy-start.2) | copy-done | bytes 4120
  2.4 0.0 copy-start.3
  2.4 0.7 %copy-done.3 = s32[2,64]{1,0:T(2,128)S(1)} copy-done((s32[2,64]{1,0:T(2,128)S(1)}, s32[2,64]{1,0:T(2,128)}, u32[]{:S(2)}) %copy-start.3) | copy-done | bytes 536
  3.0 0.0 copy-start.4
  3.0 0.7 %copy-done.4 = s32[2]{0:T(128)S(1)} copy-done((s32[2]{0:T(128)S(1)}, s32[2]{0:T(128)}, u32[]{:S(2)}) %copy-start.4) | copy-done | bytes 32
  3.7 53.5 %shard_map.55 = f32[8,8,128]{2,1,0:T(8,128)S(1)} custom-call(s32[2]{0:T(128)S(1)} %copy-done.4, s32[2,64]{1,0:T(2,128)S(1)} %copy-done.3, bf16[8,1024]{1,0:T(8,128)(2,1)S(1)} %copy-done.1, bf16[2,8,128]{2,1,0:T(8,128)(2,1)S(1)} %copy-done.2, bf16[2,2,256,128]{3,2,1,0:T(8,128)(2,1)S(1)} %copy-done), custom_call_target="tpu_custom_call" | custom-call | tf_op jit(solution)/shard_map/pallas_call | solution.py:234
  57.2 0.6 %convert_element_type.15 = bf16[1,8192]{1,0:T(2,128)(2,1)} reshape(bf16[8,8,128]{2,1,0:T(8,128)(2,1)S(1)} %convert_element_type.14) | data formatting | bytes 32768 | tf_op jit(solution)/shard_map/convert_element_type | solution.py:264
  (1 shorter events, 0.0 us)
Async XLA Ops:
  0.0 0.9 %copy-start = (bf16[2,2,256,128]{3,2,1,0:T(8,128)(2,1)S(1)}, bf16[2,2,256,128]{3,2,1,0:T(8,128)(2,1)}, u32[]{:S(2)}) copy-start(bf16[2,2,256,128]{3,2,1,0:T(8,128)(2,1)} %cache_ref.1) | copy-start | bytes 786436
  1.0 0.7 %copy-start.1 = (bf16[8,1024]{1,0:T(8,128)(2,1)S(1)}, bf16[8,1024]{1,0:T(8,128)(2,1)}, u32[]{:S(2)}) copy-start(bf16[8,1024]{1,0:T(8,128)(2,1)} %q_ref.1) | copy-start | bytes 49156
  1.7 0.7 %copy-start.2 = (bf16[2,8,128]{2,1,0:T(8,128)(2,1)S(1)}, bf16[2,8,128]{2,1,0:T(8,128)(2,1)}, u32[]{:S(2)}) copy-start(bf16[2,8,128]{2,1,0:T(8,128)(2,1)} %new_ref.1) | copy-start | bytes 12292
  2.4 0.7 %copy-start.3 = (s32[2,64]{1,0:T(2,128)S(1)}, s32[2,64]{1,0:T(2,128)}, u32[]{:S(2)}) copy-start(s32[2,64]{1,0:T(2,128)} %slot_ref.1) | copy-start | bytes 1540
  3.0 0.7 %copy-start.4 = (s32[2]{0:T(128)S(1)}, s32[2]{0:T(128)}, u32[]{:S(2)}) copy-start(s32[2]{0:T(128)} %lens_ref.1) | copy-start | bytes 28

commit v2 on v1

v2 whole, which is shorter than its diff:
```python
import functools

import jax
import jax.numpy as jnp
from jax import lax
from jax.experimental import pallas as pl
from jax.experimental.pallas import tpu as pltpu
from jax.sharding import PartitionSpec as P

HEAD_DIM = 128
PAGE = 256
SLOTS = 2
XS = 4
ZS = 16
MASKED = -1e30
FLOOR = -1e20
LOG2E = 1.4426950408889634
MESH = pl.DeviceIdType.MESH
F32 = jnp.float32
BF16 = jnp.bfloat16

NEAR = (1, -1, 2, -2)
FAR = 5
UP = (8, 7, 6, 4, 3)
DOWN = (-7, -6, -4, -3)
GROUPS = ((7, 6, 4, 3), (-7, -6, -4, -3), (8, 5, -5, 0), (2, -2, 1, -1))
PARTNERS = (1, -1, 2, -2, 3, -3, 5, -5)


def merge(diagonal, terms):
    top = functools.reduce(jnp.maximum, [stat for _, stat in terms])
    shares = [jnp.exp2(stat - top) for _, stat in terms]
    share_sum = functools.reduce(jnp.add, shares)
    merged = None
    for (values, _), share in zip(terms, shares):
        share = jnp.broadcast_to(share / share_sum, diagonal.shape)
        share = jnp.sum(jnp.where(diagonal, share, 0.0), axis=1, keepdims=True)
        term = share * values.astype(F32)
        merged = term if merged is None else merged + term
    return merged, top + jnp.log2(share_sum)


def kernel(
    hs, rows, group, lens_hbm, slot_hbm, q_hbm, new_hbm, cache_hbm, out_ref,
    lens, table, q_in, kv_all, new_all, q_all, part, part_stat, mid, mid_stat, got, got_stat,
    relay, relay_stat, bias, fin, heads,
    local_sem, kv_send, kv_recv, new_send, new_recv, q_send, q_recv,
    out_send, stat_send, mid_recv, mid_stat_recv, got_recv, got_stat_recv, head_send, head_recv,
):
    ctx = lax.axis_index("ctx")
    head = lax.axis_index("head")
    x, z = ctx // ZS, ctx % ZS
    side = x // (XS // 2)
    block = rows * group
    per = rows // hs * group
    sent = []

    def x_at(k):
        return lax.rem(x + k + XS, XS)

    def z_at(k):
        return lax.rem(z + k + ZS, ZS)

    def at_x(k):
        return (x_at(k) * ZS + z, head)

    def at_z(k):
        return (x * ZS + z_at(k), head)

    def at_head(k):
        return (ctx, lax.rem(head + k, hs))

    def send(src, dst, send_sem, recv_sem, device):
        copy = pltpu.make_async_remote_copy(
            src, dst, send_sem, recv_sem, device_id=device, device_id_type=MESH
        )
        copy.start()
        sent.append(copy)

    def arrived(ref, sem):
        pltpu.make_async_copy(ref, ref, sem).wait()

    loads = [
        pltpu.make_async_copy(q_hbm, q_in, local_sem.at[0]),
        pltpu.make_async_copy(cache_hbm, kv_all.at[0], local_sem.at[1]),
        pltpu.make_async_copy(new_hbm, new_all.at[0], local_sem.at[2]),
        pltpu.make_async_copy(slot_hbm, table, local_sem.at[3]),
        pltpu.make_async_copy(lens_hbm, lens, local_sem.at[4]),
    ]
    for load in loads:
        load.start()

    barrier = pltpu.get_barrier_semaphore()
    partners = [at_x(k) for k in range(1, XS)] + [at_z(k) for k in PARTNERS]
    partners += [at_head(k) for k in range(1, hs)]
    for device in partners:
        pl.semaphore_signal(barrier, inc=1, device_id=device, device_id_type=MESH)

    loads[0].wait()
    queries = q_in[...].astype(F32)
    queries = jnp.concatenate(
        [queries[:, h * HEAD_DIM:(h + 1) * HEAD_DIM] for h in range(group)], axis=0
    )
    q_all[0] = queries.astype(BF16)

    pl.semaphore_wait(barrier, len(partners))

    def send_queries(held, offset):
        there = (held + offset) % ZS
        send(q_all.at[held % ZS], q_all.at[there], q_send.at[there], q_recv.at[there], at_z(offset))

    def send_pages(src, held, slot, offset, number):
        there = (held + offset) % XS
        send(src, kv_all.at[there, :, slot], kv_send.at[number], kv_recv.at[there, slot], at_x(offset))

    for offset in (FAR, -FAR) + NEAR[::-1]:
        send_queries(0, offset)
    send_pages(cache_hbm.at[:, 0], 0, 0, 1, 0)
    send_pages(cache_hbm.at[:, 1], 0, 1, -1, 1)
    send_pages(cache_hbm.at[:, 1], 0, 1, 1, 2)
    send_pages(cache_hbm.at[:, 0], 0, 0, -1, 3)
    for k in range(1, XS):
        send(new_hbm, new_all.at[k], new_send.at[k], new_recv.at[k], at_x(k))

    for load in loads[1:]:
        load.wait()
    pages = table.shape[1]
    page_ids = lax.broadcasted_iota(jnp.int32, (1, pages), 1)
    live = jnp.clip(lens[side] - page_ids * PAGE, 0, PAGE).astype(F32)
    slots = lax.broadcasted_iota(jnp.int32, (XS * SLOTS, pages), 0)
    slots = SLOTS * (lax.rem(x + XS - slots // SLOTS, XS) * ZS + z) + slots % SLOTS
    live = jnp.where(table[pl.ds(side, 1), :] == slots, live, 0.0)
    live = jnp.sum(live, axis=1, keepdims=True)
    offsets = lax.broadcasted_iota(jnp.int32, (XS * SLOTS, PAGE), 1).astype(F32)
    bias[...] = jnp.where(offsets < live, 0.0, MASKED)

    arrived(q_all.at[FAR], q_recv.at[FAR])
    for offset in (3, 2, -2, 1, -1):
        send_queries(FAR, offset)
    arrived(q_all.at[ZS - FAR], q_recv.at[ZS - FAR])
    for offset in (2, -2, 1, -1):
        send_queries(-FAR, offset)
    arrived(kv_all.at[1, :, 0], kv_recv.at[1, 0])
    send_pages(kv_all.at[1, :, 0], 1, 0, 1, 4)
    arrived(kv_all.at[XS - 1, :, 1], kv_recv.at[XS - 1, 1])
    send_pages(kv_all.at[XS - 1, :, 1], -1, 1, -1, 5)

    for d in range(1, ZS):
        if d not in (FAR, ZS - FAR):
            arrived(q_all.at[d], q_recv.at[d])
    for k in range(1, XS):
        arrived(new_all.at[k], new_recv.at[k])
    new_keys = jnp.concatenate([new_all[i, 0].astype(F32) for i in range(XS)], axis=0).astype(BF16)
    new_values = jnp.concatenate([new_all[i, 1].astype(F32) for i in range(XS)], axis=0).astype(BF16)
    fresh = XS * rows
    wide = len(GROUPS[0]) * block
    new_at = lax.broadcasted_iota(jnp.int32, (block, fresh), 1)
    new_rows = rows * (lax.rem(x + XS - new_at // rows, XS) * ZS + z) + new_at % rows
    at = lax.broadcasted_iota(jnp.int32, (block, fresh), 0) % rows
    scale = HEAD_DIM ** (-0.5) * LOG2E
    contract = (((1,), (1,)), ((), ()))
    ones = jnp.ones((SLOTS * PAGE, HEAD_DIM), BF16)
    diagonal = (
        lax.broadcasted_iota(jnp.int32, (block, HEAD_DIM), 0)
        == lax.broadcasted_iota(jnp.int32, (block, HEAD_DIM), 1)
    )
    masks = [
        jnp.concatenate([bias[SLOTS * i + j:SLOTS * i + j + 1, :] for j in range(SLOTS)], axis=1)
        for i in range(XS)
    ]
    for i, slot in ((1, 1), (XS - 1, 0), (2, 0), (2, 1)):
        arrived(kv_all.at[i, :, slot], kv_recv.at[i, slot])

    def attend(members):
        mine = jnp.concatenate([q_all[-d % ZS] for d in members], axis=0)
        scores = []
        for i in range(XS):
            keys = kv_all[i, 0].reshape(SLOTS * PAGE, HEAD_DIM)
            raw = lax.dot_general(mine, keys, contract, preferred_element_type=F32)
            scores.append(raw + masks[i])
        raw = lax.dot_general(mine, new_keys, contract, preferred_element_type=F32)
        seen = [
            (new_rows <= rows * (x * ZS + z_at(d)) + at) & (new_rows >= side * (XS // 2 * ZS * rows))
            for d in members
        ]
        scores.append(raw + jnp.concatenate([jnp.where(s, 0.0, MASKED) for s in seen], axis=0))
        tiles = [
            s[:, j:j + HEAD_DIM] for s in scores[:XS] for j in range(0, SLOTS * PAGE, HEAD_DIM)
        ]
        top = jnp.max(functools.reduce(jnp.maximum, tiles), axis=1, keepdims=True)
        top = jnp.maximum(top, jnp.max(scores[XS], axis=1, keepdims=True))
        top = jnp.maximum(top, FLOOR) * scale
        total = jnp.zeros((wide, 2 * HEAD_DIM), F32)
        for i in range(XS):
            weights = jnp.exp2(scores[i] * scale - top).astype(BF16)
            values = kv_all[i, 1].reshape(SLOTS * PAGE, HEAD_DIM)
            total += jnp.dot(
                weights, jnp.concatenate([values, ones], axis=1), preferred_element_type=F32
            )
        weights = jnp.exp2(scores[XS] * scale - top).astype(BF16)
        total += jnp.dot(
            weights, jnp.concatenate([new_values, ones[:fresh]], axis=1), preferred_element_type=F32
        )
        amount = total[:, HEAD_DIM:]
        full = jnp.maximum(amount, 1.0)
        normal = (total[:, :HEAD_DIM] / full).astype(BF16)
        stat = jnp.where(amount > 0.0, top + jnp.log2(full), MASKED)
        for j, d in enumerate(members):
            part[d % ZS] = normal[j * block:(j + 1) * block]
            part_stat[d % ZS] = jnp.sum(
                jnp.where(diagonal, stat[j * block:(j + 1) * block], 0.0), axis=0, keepdims=True
            )

    def send_part(d, offset, dst, dst_stat, recv, stat_recv, slot):
        number = d % ZS
        send(part.at[number], dst.at[slot], out_send.at[number], recv.at[slot], at_z(offset))
        send(
            part_stat.at[number], dst_stat.at[slot], stat_send.at[number], stat_recv.at[slot],
            at_z(offset),
        )

    mid_slots = {d: i for i, d in enumerate(UP + DOWN)}
    got_slots = {d: i for i, d in enumerate(NEAR + (FAR, -FAR))}
    for members in GROUPS:
        attend(members)
        for d in members:
            if d in mid_slots:
                offset = d - FAR if d > 0 else d + FAR
                send_part(d, offset, mid, mid_stat, mid_recv, mid_stat_recv, mid_slots[d])
            elif d in NEAR:
                send_part(d, d, got, got_stat, got_recv, got_stat_recv, got_slots[d])

    for number, (d, others) in enumerate(((FAR, UP), (-FAR, DOWN))):
        terms = [(part[d % ZS], part_stat[d % ZS])]
        for other in others:
            slot = mid_slots[other]
            arrived(mid.at[slot], mid_recv.at[slot])
            arrived(mid_stat.at[slot], mid_stat_recv.at[slot])
            terms.append((mid[slot], mid_stat[slot]))
        merged, stat = merge(diagonal, terms)
        relay[number] = merged.astype(BF16)
        relay_stat[number] = stat
        slot = got_slots[d]
        send(relay.at[number], got.at[slot], out_send.at[d % ZS], got_recv.at[slot], at_z(d))
        send(
            relay_stat.at[number], got_stat.at[slot], stat_send.at[d % ZS], got_stat_recv.at[slot],
            at_z(d),
        )

    terms = [(part[0], part_stat[0])]
    for slot in got_slots.values():
        arrived(got.at[slot], got_recv.at[slot])
        arrived(got_stat.at[slot], got_stat_recv.at[slot])
        terms.append((got[slot], got_stat[slot]))
    merged, _ = merge(diagonal, terms)
    for h in range(group):
        fin[pl.ds(h, rows, stride=group), :] = merged[h * rows:(h + 1) * rows]

    def fin_at(there):
        return pl.ds(pl.multiple_of(there * per, 8), per)

    for k in range(1, hs):
        there = lax.rem(head + k, hs)
        send(
            fin.at[fin_at(there), :], heads.at[head], head_send.at[k], head_recv.at[head], at_head(k)
        )
    heads[head] = fin[fin_at(head), :]
    for k in range(1, hs):
        there = lax.rem(head + k, hs)
        arrived(heads.at[there], head_recv.at[there])
    out_ref[...] = heads[...]
    for copy in sent:
        copy.wait_send()


def local(hs, prefix_len, page_slot, queries, new_kv, cache):
    rows = queries.shape[0]
    group = queries.shape[1] // HEAD_DIM
    block = rows * group
    per = rows // hs * group
    mids = len(UP + DOWN)
    gots = len(NEAR) + 2
    dma = pltpu.SemaphoreType.DMA
    result = pl.pallas_call(
        functools.partial(kernel, hs, rows, group),
        out_shape=jax.ShapeDtypeStruct((hs, per, HEAD_DIM), F32),
        in_specs=[pl.BlockSpec(memory_space=pltpu.HBM)] * 5,
        out_specs=pl.BlockSpec(memory_space=pltpu.VMEM),
        scratch_shapes=[
            pltpu.SMEM(prefix_len.shape, jnp.int32),
            pltpu.VMEM(page_slot.shape, jnp.int32),
            pltpu.VMEM(queries.shape, BF16),
            pltpu.VMEM((XS, 2, SLOTS, PAGE, HEAD_DIM), BF16),
            pltpu.VMEM((XS, 2, rows, HEAD_DIM), BF16),
            pltpu.VMEM((ZS, block, HEAD_DIM), BF16),
            pltpu.VMEM((ZS, block, HEAD_DIM), BF16),
            pltpu.VMEM((ZS, 1, HEAD_DIM), F32),
            pltpu.VMEM((mids, block, HEAD_DIM), BF16),
            pltpu.VMEM((mids, 1, HEAD_DIM), F32),
            pltpu.VMEM((gots, block, HEAD_DIM), BF16),
            pltpu.VMEM((gots, 1, HEAD_DIM), F32),
            pltpu.VMEM((2, block, HEAD_DIM), BF16),
            pltpu.VMEM((2, 1, HEAD_DIM), F32),
            pltpu.VMEM((XS * SLOTS, PAGE), F32),
            pltpu.VMEM((block, HEAD_DIM), F32),
            pltpu.VMEM((hs, per, HEAD_DIM), F32),
            dma((5,)), dma((6,)), dma((XS, SLOTS)), dma((XS,)), dma((XS,)), dma((ZS,)), dma((ZS,)),
            dma((ZS,)), dma((ZS,)), dma((mids,)), dma((mids,)), dma((gots,)), dma((gots,)),
            dma((hs,)), dma((hs,)),
        ],
        compiler_params=pltpu.CompilerParams(
            collective_id=0, has_side_effects=True, vmem_limit_bytes=62 * 2**20
        ),
    )(prefix_len, page_slot, queries, new_kv, cache.reshape(2, SLOTS, PAGE, HEAD_DIM))
    result = result.reshape(hs, rows // hs, group * HEAD_DIM)
    return result.transpose(1, 0, 2).reshape(rows // hs, hs * group * HEAD_DIM).astype(BF16)


def solution(mesh):
    return jax.shard_map(
        functools.partial(local, mesh.shape["head"]),
        mesh=mesh,
        in_specs=(P(), P(), P("ctx", "head"), P(None, "ctx", "head"), P(None, "ctx", None, "head")),
        out_specs=P(("ctx", "head"), None),
        check_vma=False,
    )
```

time: 58.1 us -> 48.7 us (0.84)
  Pallas kernels: 53.5 us -> 47.1 us
  local copies, waits for them, and re-layouts: 4.31 us -> 0.63 us
  other arithmetic: 0.01 us -> 0.76 us
    pallas_call x1, Pallas kernels: 53.5 us -> 47.1 us  [local(): pl.pallas_call(functools.partial(kernel, hs, rows, group), out_shape=jax....]
    unnamed x10 -> x0, local copies, waits for them, and re-layouts: 3.69 us -> none
    convert_element_type x1, other arithmetic: 0.01 us -> 0.76 us  [local(): result.transpose(1, 0, 2).reshape(rows // hs, hs * group * HEAD_DIM)]
where the time goes in v2:
time: 48.7 us; the launch traced here: 48.5 us
  Pallas kernels  47.1 us (97%)
  other arithmetic  0.76 us (2%)
  local copies, waits for them, and re-layouts  0.63 us (1%)
    pallas_call x1, Pallas kernels, local(): pl.pallas_call(functools.partial(kernel, hs, rows, group), out_shape=jax....  47.1 us

profile of v2, /device:TPU:1, one launch (start us, length us, event | category | flops | bytes accessed | tf_op | source)
XLA Modules:
  0.0 48.5 jit_solution(2881720675924840683)
XLA Ops:
  0.0 47.1 %shard_map.55 = f32[8,8,128]{2,1,0:T(8,128)} custom-call(s32[2]{0:T(128)} %lens_hbm.1, s32[2,64]{1,0:T(2,128)} %slot_hbm.1, bf16[8,1024]{1,0:T(8,128)(2,1)} %q_hbm.1, bf16[2,8,128]{2,1,0:T(8,128)(2,1)} %new_hbm.1, bf16[2,2,256,128]{3,2,1,0:T(8,128)(2,1)} %cache_hbm.1), custom_call_target="tpu_custom_call" | custom-call | tf_op jit(solution)/shard_map/pallas_call | solution.py:284
  47.1 0.8 %convert_element_type.14 = bf16[8,8,128]{2,1,0:T(8,128)(2,1)S(1)} convert(f32[8,8,128]{2,1,0:T(8,128)} %shard_map.55) | non-fusion elementwise | flops 8192 | bytes 49152 | tf_op jit(solution)/shard_map/convert_element_type | solution.py:316
  47.9 0.6 %convert_element_type.15 = bf16[1,8192]{1,0:T(2,128)(2,1)} reshape(bf16[8,8,128]{2,1,0:T(8,128)(2,1)S(1)} %convert_element_type.14) | data formatting | bytes 32768 | tf_op jit(solution)/shard_map/convert_element_type | solution.py:316

commit v3 on v2

v3 whole, which is shorter than its diff:
```python
import functools

import jax
import jax.numpy as jnp
from jax import lax
from jax.experimental import pallas as pl
from jax.experimental.pallas import tpu as pltpu
from jax.sharding import PartitionSpec as P

HEAD_DIM = 128
PAGE = 256
SLOTS = 2
XS = 4
ZS = 16
MASKED = -1e30
FLOOR = -1e20
LOG2E = 1.4426950408889634
MESH = pl.DeviceIdType.MESH
F32 = jnp.float32
BF16 = jnp.bfloat16

NEAR = (2, -2, 1, -1)
FAR = 5
HALF = 8
RELAY = HALF - FAR
SETS = {t: (t, t - FAR, t + FAR) for t in NEAR}
ORDER = sum(SETS.values(), ()) + (-FAR, FAR, 0, HALF)
FIRST = (NEAR, (0, -FAR, FAR), (-3, 7, -7, 3, HALF), (-4, 6, -6, 4))
SECOND = (FIRST[2], FIRST[3], FIRST[1], FIRST[0])
PARTNERS = (1, -1, 2, -2, RELAY, -RELAY, FAR, -FAR)


def merge(diagonal, terms):
    top = functools.reduce(jnp.maximum, [stat for _, stat in terms])
    shares = [jnp.exp2(stat - top) for _, stat in terms]
    share_sum = functools.reduce(jnp.add, shares)
    merged = None
    for (values, _), share in zip(terms, shares):
        share = jnp.broadcast_to(share / share_sum, diagonal.shape)
        share = jnp.sum(jnp.where(diagonal, share, 0.0), axis=1, keepdims=True)
        term = share * values.astype(F32)
        merged = term if merged is None else merged + term
    return merged, top + jnp.log2(share_sum)


def kernel(
    hs, rows, group, lens_hbm, slot_hbm, q_hbm, new_hbm, cache_hbm, out_ref,
    lens, table, q_in, kv_all, new_all, q_all, part, part_stat, box, box_stat, pair, pair_stat,
    half, half_stat, final, final_stat, last, last_stat, tops, totals, bias, wide, heads,
    local_sem, kv_send, kv_recv, new_send, new_recv, q_send, q_recv, out_send, stat_send,
    pair_send, pair_stat_send, box_recv, box_stat_recv, pair_recv, pair_stat_recv, half_recv,
    last_send, last_stat_send, last_recv, last_stat_recv,
):
    ctx = lax.axis_index("ctx")
    head = lax.axis_index("head")
    x, z = ctx // ZS, ctx % ZS
    side = x // (XS // 2)
    block = rows * group
    own = rows // hs
    sent = []
    at_slot = {d: i for i, d in enumerate(ORDER)}

    def z_at(k):
        return lax.rem(z + k + ZS, ZS)

    def at_x(k):
        return (lax.rem(x + k + XS, XS) * ZS + z, head)

    def at_z(k):
        return (x * ZS + z_at(k), head)

    def at_head(k):
        return (ctx, lax.rem(head + k, hs))

    def send(src, dst, send_sem, recv_sem, device):
        copy = pltpu.make_async_remote_copy(
            src, dst, send_sem, recv_sem, device_id=device, device_id_type=MESH
        )
        copy.start()
        sent.append(copy)

    def arrived(ref, sem):
        pltpu.make_async_copy(ref, ref, sem).wait()

    barrier = pltpu.get_barrier_semaphore()
    partners = [at_x(k) for k in range(1, XS)] + [at_z(k) for k in PARTNERS]
    partners += [at_head(k) for k in range(1, hs)]
    for device in partners:
        pl.semaphore_signal(barrier, inc=1, device_id=device, device_id_type=MESH)

    loads = [
        pltpu.make_async_copy(q_hbm, q_in, local_sem.at[0]),
        pltpu.make_async_copy(cache_hbm, kv_all.at[0], local_sem.at[1]),
        pltpu.make_async_copy(new_hbm, new_all.at[0], local_sem.at[2]),
        pltpu.make_async_copy(slot_hbm, table, local_sem.at[3]),
        pltpu.make_async_copy(lens_hbm, lens, local_sem.at[4]),
    ]
    for load in loads:
        load.start()

    pl.semaphore_wait(barrier, len(partners))

    def send_pages(src, held, slot, offset, number):
        there = (held + offset) % XS
        send(src, kv_all.at[there, :, slot], kv_send.at[number], kv_recv.at[there, slot], at_x(offset))

    send_pages(cache_hbm.at[:, 0], 0, 0, 1, 0)
    send_pages(cache_hbm.at[:, 1], 0, 1, -1, 1)
    send_pages(cache_hbm.at[:, 1], 0, 1, 1, 2)
    send_pages(cache_hbm.at[:, 0], 0, 0, -1, 3)

    def slot_of(d, count=1):
        return pl.ds(at_slot[d], count)

    def send_queries(src, dst, count, offset):
        dst = slot_of(dst, count)
        number = at_slot[offset] if count == 1 else at_slot[offset] + 1
        recv = at_slot[-offset] if count == 1 else at_slot[-offset] + 1
        send(q_all.at[slot_of(src, count)], q_all.at[dst], q_send.at[number], q_recv.at[recv], at_z(offset))

    def queries_arrived(d, count=1):
        arrived(q_all.at[slot_of(d, count)], q_recv.at[at_slot[d]])

    loads[0].wait()
    queries = q_in[...].astype(F32)
    for h in range(group):
        wide[pl.ds(h, rows, stride=group), :] = queries[:, h * HEAD_DIM:(h + 1) * HEAD_DIM]
    q_all[at_slot[0]] = wide[...].astype(BF16)
    for offset in (FAR, -FAR) + NEAR:
        send_queries(0, -offset, 1, offset)
    for k in range(1, XS):
        send(new_hbm, new_all.at[k], new_send.at[k], new_recv.at[k], at_x(k))

    for load in loads[1:]:
        load.wait()
    pages = table.shape[1]
    page_ids = lax.broadcasted_iota(jnp.int32, (1, pages), 1)
    live = jnp.clip(lens[side] - page_ids * PAGE, 0, PAGE).astype(F32)
    slots = lax.broadcasted_iota(jnp.int32, (XS * SLOTS, pages), 0)
    slots = SLOTS * (lax.rem(x + XS - slots // SLOTS, XS) * ZS + z) + slots % SLOTS
    live = jnp.where(table[pl.ds(side, 1), :] == slots, live, 0.0)
    live = jnp.sum(live, axis=1, keepdims=True)
    offsets = lax.broadcasted_iota(jnp.int32, (XS * SLOTS, PAGE), 1).astype(F32)
    bias[...] = jnp.where(offsets < live, 0.0, MASKED)

    arrived(kv_all.at[1, :, 0], kv_recv.at[1, 0])
    send_pages(kv_all.at[1, :, 0], 1, 0, 1, 4)
    arrived(kv_all.at[XS - 1, :, 1], kv_recv.at[XS - 1, 1])
    send_pages(kv_all.at[XS - 1, :, 1], -1, 1, -1, 5)
    queries_arrived(-FAR)
    send(
        q_all.at[slot_of(-FAR)], q_all.at[slot_of(HALF)], q_send.at[at_slot[HALF]],
        q_recv.at[at_slot[HALF]], at_z(RELAY),
    )
    queries_arrived(FAR)
    for offset in NEAR:
        send_queries(-FAR, SETS[-offset][1], 2, offset)

    for k in range(1, XS):
        arrived(new_all.at[k], new_recv.at[k])
    new_keys = jnp.concatenate([new_all[i, 0].astype(F32) for i in range(XS)], axis=0).astype(BF16)
    new_values = jnp.concatenate([new_all[i, 1].astype(F32) for i in range(XS)], axis=0).astype(BF16)
    fresh = XS * rows
    new_at = lax.broadcasted_iota(jnp.int32, (block, fresh), 1)
    new_rows = rows * (lax.rem(x + XS - new_at // rows, XS) * ZS + z) + new_at % rows
    at = lax.broadcasted_iota(jnp.int32, (block, fresh), 0) // group
    scale = HEAD_DIM ** (-0.5) * LOG2E
    contract = (((1,), (1,)), ((), ()))
    ones = jnp.ones((SLOTS * PAGE, HEAD_DIM), BF16)
    diagonal = (
        lax.broadcasted_iota(jnp.int32, (block, HEAD_DIM), 0)
        == lax.broadcasted_iota(jnp.int32, (block, HEAD_DIM), 1)
    )

    def gathered(members):
        return jnp.concatenate([q_all[at_slot[d]] for d in members], axis=0)

    def score(mine, i):
        keys = kv_all[i, 0].reshape(SLOTS * PAGE, HEAD_DIM)
        raw = lax.dot_general(mine, keys, contract, preferred_element_type=F32)
        return raw + jnp.concatenate(
            [bias[SLOTS * i + j:SLOTS * i + j + 1, :] for j in range(SLOTS)], axis=1
        )

    def highest(scores):
        tiles = [s[:, j:j + HEAD_DIM] for s in scores for j in range(0, SLOTS * PAGE, HEAD_DIM)]
        return jnp.max(functools.reduce(jnp.maximum, tiles), axis=1, keepdims=True)

    def weigh(scores, top, i):
        weights = jnp.exp2(scores * scale - top).astype(BF16)
        values = kv_all[i, 1].reshape(SLOTS * PAGE, HEAD_DIM)
        return jnp.dot(
            weights, jnp.concatenate([values, ones], axis=1), preferred_element_type=F32
        )

    def attend_first(members):
        mine = gathered(members)
        here = (0, 1, XS - 1)
        scores = [score(mine, i) for i in here]
        raw = lax.dot_general(mine, new_keys, contract, preferred_element_type=F32)
        seen = [
            (new_rows <= rows * (x * ZS + z_at(d)) + at) & (new_rows >= side * (XS // 2 * ZS * rows))
            for d in members
        ]
        new_scores = raw + jnp.concatenate([jnp.where(s, 0.0, MASKED) for s in seen], axis=0)
        top = jnp.maximum(highest(scores), jnp.max(new_scores, axis=1, keepdims=True))
        top = jnp.maximum(top, FLOOR) * scale
        weights = jnp.exp2(new_scores * scale - top).astype(BF16)
        total = jnp.dot(
            weights, jnp.concatenate([new_values, ones[:fresh]], axis=1), preferred_element_type=F32
        )
        for i, s in zip(here, scores):
            total += weigh(s, top, i)
        top = jnp.broadcast_to(top, (top.shape[0], HEAD_DIM))
        for j, d in enumerate(members):
            tops[at_slot[d]] = top[j * block:(j + 1) * block]
            totals[at_slot[d]] = total[j * block:(j + 1) * block]

    def attend_second(members):
        scores = score(gathered(members), 2)
        before = jnp.concatenate([tops[at_slot[d]] for d in members], axis=0)
        total = jnp.concatenate([totals[at_slot[d]] for d in members], axis=0)
        top = jnp.maximum(before, highest([scores]) * scale)
        fade = jnp.exp2(before - top)
        total = total * jnp.concatenate([fade, fade], axis=1)
        total += weigh(scores, top[:, :1], 2)
        amount = total[:, HEAD_DIM:]
        full = jnp.maximum(amount, 1.0)
        normal = (total[:, :HEAD_DIM] / full).astype(BF16)
        stat = jnp.where(amount > 0.0, top + jnp.log2(full), MASKED)
        for j, d in enumerate(members):
            part[at_slot[d]] = normal[j * block:(j + 1) * block]
            part_stat[at_slot[d]] = jnp.sum(
                jnp.where(diagonal, stat[j * block:(j + 1) * block], 0.0), axis=0, keepdims=True
            )

    arrived(kv_all.at[1, :, 1], kv_recv.at[1, 1])
    arrived(kv_all.at[XS - 1, :, 0], kv_recv.at[XS - 1, 0])
    for t in NEAR:
        queries_arrived(t)
    attend_first(FIRST[0])
    attend_first(FIRST[1])
    queries_arrived(HALF)
    for t in NEAR:
        queries_arrived(SETS[t][1], 2)
    attend_first(FIRST[2])
    attend_first(FIRST[3])
    for slot in range(SLOTS):
        arrived(kv_all.at[2, :, slot], kv_recv.at[2, slot])

    def send_parts(d, count, dst, dst_stat, data_sems, stat_sems, offset):
        send(part.at[slot_of(d, count)], dst, *data_sems, at_z(offset))
        send(part_stat.at[slot_of(d, count)], dst_stat, *stat_sems, at_z(offset))

    def send_pair(t):
        here, there = NEAR.index(t), NEAR.index(-t)
        send_parts(
            SETS[t][1], 2, pair.at[there], pair_stat.at[there],
            (pair_send.at[here], pair_recv.at[there]),
            (pair_stat_send.at[here], pair_stat_recv.at[there]), t,
        )

    def send_near(t):
        here, there = NEAR.index(t), NEAR.index(-t)
        send_parts(
            t, 1, box.at[pl.ds(there, 1)], box_stat.at[pl.ds(there, 1)],
            (out_send.at[here], box_recv.at[there]), (stat_send.at[here], box_stat_recv.at[there]), t,
        )

    attend_second(SECOND[0])
    send_parts(
        HALF, 1, half, half_stat, (out_send.at[4], half_recv.at[0]),
        (stat_send.at[4], half_recv.at[1]), RELAY,
    )
    send_pair(2)
    send_pair(-2)
    attend_second(SECOND[1])
    send_pair(1)
    send_pair(-1)
    attend_second(SECOND[2])
    attend_second(SECOND[3])
    for t in NEAR:
        send_near(t)

    def send_final(number, offset, k):
        there = lax.rem(head + k, hs)
        device = (x * ZS + z_at(offset), there)
        send(
            final.at[number, pl.ds(there * own, own)], last.at[number, head],
            last_send.at[number, k], last_recv.at[number, head], device,
        )
        send(
            final_stat.at[number], last_stat.at[number, head],
            last_stat_send.at[number, k], last_stat_recv.at[number, head], device,
        )

    for i in range(len(NEAR)):
        arrived(pair.at[i], pair_recv.at[i])
        arrived(pair_stat.at[i], pair_stat_recv.at[i])
    for number, d in enumerate((-FAR, FAR)):
        terms = [(part[at_slot[d]], part_stat[at_slot[d]])]
        terms += [(pair[i, number], pair_stat[i, number]) for i in range(len(NEAR))]
        if d == FAR:
            arrived(half, half_recv.at[0])
            arrived(half_stat, half_recv.at[1])
            terms.append((half[0], half_stat[0]))
        merged, stat = merge(diagonal, terms)
        final[1 + number] = merged.astype(BF16).reshape(rows, group, HEAD_DIM)
        final_stat[1 + number] = stat
        for k in range(hs):
            send_final(1 + number, d, k)
    terms = [(part[at_slot[0]], part_stat[at_slot[0]])]
    for i in range(len(NEAR)):
        arrived(box.at[i], box_recv.at[i])
        arrived(box_stat.at[i], box_stat_recv.at[i])
        terms.append((box[i], box_stat[i]))
    merged, stat = merge(diagonal, terms)
    final[0] = merged.astype(BF16).reshape(rows, group, HEAD_DIM)
    final_stat[0] = stat
    for k in range(1, hs):
        send_final(0, 0, k)
    last[0, head] = final[0, pl.ds(head * own, own)]
    last_stat[0, head] = stat
    for copy in sent:
        copy.wait_send()
    for number in range(3):
        for k in range(0 if number else 1, hs):
            there = lax.rem(head + k, hs)
            arrived(last.at[number, there], last_recv.at[number, there])
            arrived(last_stat.at[number, there], last_stat_recv.at[number, there])
    mine = (own * group, HEAD_DIM)
    diagonal = (
        lax.broadcasted_iota(jnp.int32, mine, 0) + head * own * group
        == lax.broadcasted_iota(jnp.int32, mine, 1)
    )
    for g in range(hs):
        terms = [(last[number, g].reshape(mine), last_stat[number, g]) for number in range(3)]
        heads[g] = merge(diagonal, terms)[0]
    for i in range(own):
        pieces = [heads[g, i * group + h:i * group + h + 1, :] for g in range(hs) for h in range(group)]
        out_ref[i:i + 1, :] = jnp.concatenate(pieces, axis=1).astype(BF16)


def local(hs, prefix_len, page_slot, queries, new_kv, cache):
    rows = queries.shape[0]
    group = queries.shape[1] // HEAD_DIM
    block = rows * group
    own = rows // hs
    near = len(NEAR)
    dma = pltpu.SemaphoreType.DMA
    return pl.pallas_call(
        functools.partial(kernel, hs, rows, group),
        out_shape=jax.ShapeDtypeStruct((rows // hs, hs * group * HEAD_DIM), BF16),
        in_specs=[pl.BlockSpec(memory_space=pltpu.HBM)] * 5,
        out_specs=pl.BlockSpec(memory_space=pltpu.VMEM),
        scratch_shapes=[
            pltpu.SMEM(prefix_len.shape, jnp.int32),
            pltpu.VMEM(page_slot.shape, jnp.int32),
            pltpu.VMEM(queries.shape, BF16),
            pltpu.VMEM((XS, 2, SLOTS, PAGE, HEAD_DIM), BF16),
            pltpu.VMEM((XS, 2, rows, HEAD_DIM), BF16),
            pltpu.VMEM((ZS, block, HEAD_DIM), BF16),
            pltpu.VMEM((ZS, block, HEAD_DIM), BF16),
            pltpu.VMEM((ZS, 1, HEAD_DIM), F32),
            pltpu.VMEM((near, block, HEAD_DIM), BF16),
            pltpu.VMEM((near, 1, HEAD_DIM), F32),
            pltpu.VMEM((near, 2, block, HEAD_DIM), BF16),
            pltpu.VMEM((near, 2, 1, HEAD_DIM), F32),
            pltpu.VMEM((1, block, HEAD_DIM), BF16),
            pltpu.VMEM((1, 1, HEAD_DIM), F32),
            pltpu.VMEM((3, rows, group, HEAD_DIM), BF16),
            pltpu.VMEM((3, 1, HEAD_DIM), F32),
            pltpu.VMEM((3, hs, own, group, HEAD_DIM), BF16),
            pltpu.VMEM((3, hs, 1, HEAD_DIM), F32),
            pltpu.VMEM((ZS, block, HEAD_DIM), F32),
            pltpu.VMEM((ZS, block, 2 * HEAD_DIM), F32),
            pltpu.VMEM((XS * SLOTS, PAGE), F32),
            pltpu.VMEM((block, HEAD_DIM), F32),
            pltpu.VMEM((hs, own * group, HEAD_DIM), F32),
            dma((5,)), dma((6,)), dma((XS, SLOTS)), dma((XS,)), dma((XS,)), dma((ZS,)), dma((ZS,)),
            dma((near + 1,)), dma((near + 1,)), dma((near,)), dma((near,)), dma((near,)),
            dma((near,)), dma((near,)), dma((near,)), dma((2,)),
            dma((3, hs)), dma((3, hs)), dma((3, hs)), dma((3, hs)),
        ],
        compiler_params=pltpu.CompilerParams(
            collective_id=0, has_side_effects=True, vmem_limit_bytes=62 * 2**20
        ),
    )(prefix_len, page_slot, queries, new_kv, cache.reshape(2, SLOTS, PAGE, HEAD_DIM))


def solution(mesh):
    return jax.shard_map(
        functools.partial(local, mesh.shape["head"]),
        mesh=mesh,
        in_specs=(P(), P(), P("ctx", "head"), P(None, "ctx", "head"), P(None, "ctx", None, "head")),
        out_specs=P(("ctx", "head"), None),
        check_vma=False,
    )
```

time: 48.7 us -> 45.4 us (0.932)
  Pallas kernels: 47.1 us -> 43.8 us
  local copies, waits for them, and re-layouts: 0.63 us -> 1.41 us
  other arithmetic: 0.76 us -> 0 us
    pallas_call x1, Pallas kernels: 47.1 us -> 43.8 us  [local(): pl.pallas_call(functools.partial(kernel, hs, rows, group), out_shape=jax....]
    unnamed x0 -> x1, local copies, waits for them, and re-layouts: none -> 1.41 us
    convert_element_type x1 -> x0, other arithmetic: 0.76 us -> none  [local(): result.transpose(1, 0, 2).reshape(rows // hs, hs * group * HEAD_DIM)]
    convert_element_type x1 -> x0, local copies, waits for them, and re-layouts: 0.63 us -> none  [local(): result.transpose(1, 0, 2).reshape(rows // hs, hs * group * HEAD_DIM)]
where the time goes in v3:
time: 45.4 us; the launch traced here: 45.2 us
  Pallas kernels  43.8 us (96%)
  local copies, waits for them, and re-layouts  1.41 us (3%)
    pallas_call x1, Pallas kernels, local(): pl.pallas_call(functools.partial(kernel, hs, rows, group), out_shape=jax....  43.8 us
    unnamed x1, local copies, waits for them, and re-layouts  1.41 us

profile of v3, /device:TPU:1, one launch (start us, length us, event | category | flops | bytes accessed | tf_op | source)
XLA Modules:
  0.0 45.2 jit_solution(15882034123898440617)
XLA Ops:
  0.0 43.8 %shard_map.55 = bf16[1,8192]{1,0:T(2,128)(2,1)} custom-call(s32[2]{0:T(128)} %lens_hbm.1, s32[2,64]{1,0:T(2,128)} %slot_hbm.1, bf16[8,1024]{1,0:T(8,128)(2,1)} %q_hbm.1, bf16[2,8,128]{2,1,0:T(8,128)(2,1)} %new_hbm.1, bf16[2,2,256,128]{3,2,1,0:T(8,128)(2,1)} %cache_hbm.1), custom_call_target="tpu_custom_call" | custom-call | tf_op jit(solution)/shard_map/pallas_call | solution.py:351
  43.8 1.4 %copy.7 = bf16[1,8192]{1,0:T(2,128)(2,1)} copy(bf16[1,8192]{1,0:T(2,128)(2,1)} %shard_map.55) | data formatting | bytes 32768

commit v4 on v3

--- a/solution.py
+++ b/solution.py
@@ -383,9 +383,9 @@
             dma((3, hs)), dma((3, hs)), dma((3, hs)), dma((3, hs)),
         ],
         compiler_params=pltpu.CompilerParams(
-            collective_id=0, has_side_effects=True, vmem_limit_bytes=62 * 2**20
+            collective_id=0, has_side_effects=True, vmem_limit_bytes=48 * 2**20
         ),
-    )(prefix_len, page_slot, queries, new_kv, cache.reshape(2, SLOTS, PAGE, HEAD_DIM))
+    )(*[pltpu.with_memory_space_constraint(a, pltpu.HBM) for a in (prefix_len, page_slot, queries, new_kv, cache.reshape(2, SLOTS, PAGE, HEAD_DIM))])
 
 
 def solution(mesh):

time: 45.4 us -> 43.9 us (0.967)
  local copies, waits for them, and re-layouts: 1.41 us -> 0.62 us
  Pallas kernels: 43.8 us -> 43.2 us
    unnamed x1, local copies, waits for them, and re-layouts: 1.41 us -> 0.62 us
    pallas_call x1, Pallas kernels: 43.8 us -> 43.2 us  [local(): pl.pallas_call(functools.partial(kernel, hs, rows, group), out_shape=jax....]
where the time goes in v4:
time: 43.9 us; the launch traced here: 43.8 us
  Pallas kernels  43.2 us (98%)
  local copies, waits for them, and re-layouts  0.62 us (1%)
    pallas_call x1, Pallas kernels, local(): pl.pallas_call(functools.partial(kernel, hs, rows, group), out_shape=jax....  43.2 us

profile of v4, /device:TPU:1, one launch (start us, length us, event | category | flops | bytes accessed | tf_op | source)
XLA Modules:
  0.0 43.8 jit_solution(6552071307584427736)
XLA Ops:
  0.0 43.2 %shard_map.55 = bf16[1,8192]{1,0:T(2,128)(2,1)S(1)} custom-call(s32[2]{0:T(128)} %lens_hbm.1, s32[2,64]{1,0:T(2,128)} %slot_hbm.1, bf16[8,1024]{1,0:T(8,128)(2,1)} %q_hbm.1, bf16[2,8,128]{2,1,0:T(8,128)(2,1)} %new_hbm.1, bf16[2,2,256,128]{3,2,1,0:T(8,128)(2,1)} %cache_hbm.1), custom_call_target="tpu_custom_call" | custom-call | tf_op jit(solution)/shard_map/pallas_call | solution.py:351
  43.2 0.6 %copy.7 = bf16[1,8192]{1,0:T(2,128)(2,1)} copy(bf16[1,8192]{1,0:T(2,128)(2,1)S(1)} %shard_map.55) | data formatting | bytes 32768

commit v5 on v4

--- a/solution.py
+++ b/solution.py
@@ -83,8 +83,8 @@
         pltpu.make_async_copy(ref, ref, sem).wait()
 
     barrier = pltpu.get_barrier_semaphore()
-    partners = [at_x(k) for k in range(1, XS)] + [at_z(k) for k in PARTNERS]
-    partners += [at_head(k) for k in range(1, hs)]
+    partners = [at_z(k) for k in PARTNERS] + [at_head(k) for k in range(1, hs)]
+    partners += [at_x(k) for k in range(1, XS)]
     for device in partners:
         pl.semaphore_signal(barrier, inc=1, device_id=device, device_id_type=MESH)
 
@@ -98,39 +98,11 @@
     for load in loads:
         load.start()
 
-    pl.semaphore_wait(barrier, len(partners))
-
-    def send_pages(src, held, slot, offset, number):
-        there = (held + offset) % XS
-        send(src, kv_all.at[there, :, slot], kv_send.at[number], kv_recv.at[there, slot], at_x(offset))
-
-    send_pages(cache_hbm.at[:, 0], 0, 0, 1, 0)
-    send_pages(cache_hbm.at[:, 1], 0, 1, -1, 1)
-    send_pages(cache_hbm.at[:, 1], 0, 1, 1, 2)
-    send_pages(cache_hbm.at[:, 0], 0, 0, -1, 3)
-
-    def slot_of(d, count=1):
-        return pl.ds(at_slot[d], count)
-
-    def send_queries(src, dst, count, offset):
-        dst = slot_of(dst, count)
-        number = at_slot[offset] if count == 1 else at_slot[offset] + 1
-        recv = at_slot[-offset] if count == 1 else at_slot[-offset] + 1
-        send(q_all.at[slot_of(src, count)], q_all.at[dst], q_send.at[number], q_recv.at[recv], at_z(offset))
-
-    def queries_arrived(d, count=1):
-        arrived(q_all.at[slot_of(d, count)], q_recv.at[at_slot[d]])
-
     loads[0].wait()
     queries = q_in[...].astype(F32)
     for h in range(group):
         wide[pl.ds(h, rows, stride=group), :] = queries[:, h * HEAD_DIM:(h + 1) * HEAD_DIM]
     q_all[at_slot[0]] = wide[...].astype(BF16)
-    for offset in (FAR, -FAR) + NEAR:
-        send_queries(0, -offset, 1, offset)
-    for k in range(1, XS):
-        send(new_hbm, new_all.at[k], new_send.at[k], new_recv.at[k], at_x(k))
-
     for load in loads[1:]:
         load.wait()
     pages = table.shape[1]
@@ -143,10 +115,34 @@
     offsets = lax.broadcasted_iota(jnp.int32, (XS * SLOTS, PAGE), 1).astype(F32)
     bias[...] = jnp.where(offsets < live, 0.0, MASKED)
 
-    arrived(kv_all.at[1, :, 0], kv_recv.at[1, 0])
-    send_pages(kv_all.at[1, :, 0], 1, 0, 1, 4)
-    arrived(kv_all.at[XS - 1, :, 1], kv_recv.at[XS - 1, 1])
-    send_pages(kv_all.at[XS - 1, :, 1], -1, 1, -1, 5)
+    pl.semaphore_wait(barrier, len(partners))
+
+    def send_pages(src, held, slot, offset, number):
+        there = (held + offset) % XS
+        send(src, kv_all.at[there, :, slot], kv_send.at[number], kv_recv.at[there, slot], at_x(offset))
+
+    send_pages(cache_hbm.at[:, 0], 0, 0, 1, 0)
+    send_pages(cache_hbm.at[:, 1], 0, 1, -1, 1)
+    send_pages(cache_hbm.at[:, 1], 0, 1, 1, 2)
+    send_pages(cache_hbm.at[:, 0], 0, 0, -1, 3)
+
+    def slot_of(d, count=1):
+        return pl.ds(at_slot[d], count)
+
+    def send_queries(src, dst, count, offset):
+        dst = slot_of(dst, count)
+        number = at_slot[offset] if count == 1 else at_slot[offset] + 1
+        recv = at_slot[-offset] if count == 1 else at_slot[-offset] + 1
+        send(q_all.at[slot_of(src, count)], q_all.at[dst], q_send.at[number], q_recv.at[recv], at_z(offset))
+
+    def queries_arrived(d, count=1):
+        arrived(q_all.at[slot_of(d, count)], q_recv.at[at_slot[d]])
+
+    for offset in (FAR, -FAR) + NEAR:
+        send_queries(0, -offset, 1, offset)
+    for k in range(1, XS):
+        send(new_hbm, new_all.at[k], new_send.at[k], new_recv.at[k], at_x(k))
+
     queries_arrived(-FAR)
     send(
         q_all.at[slot_of(-FAR)], q_all.at[slot_of(HALF)], q_send.at[at_slot[HALF]],
@@ -156,6 +152,10 @@
     for offset in NEAR:
         send_queries(-FAR, SETS[-offset][1], 2, offset)
 
+    arrived(kv_all.at[1, :, 0], kv_recv.at[1, 0])
+    send_pages(kv_all.at[1, :, 0], 1, 0, 1, 4)
+    arrived(kv_all.at[XS - 1, :, 1], kv_recv.at[XS - 1, 1])
+    send_pages(kv_all.at[XS - 1, :, 1], -1, 1, -1, 5)
     for k in range(1, XS):
         arrived(new_all.at[k], new_recv.at[k])
     new_keys = jnp.concatenate([new_all[i, 0].astype(F32) for i in range(XS)], axis=0).astype(BF16)
@@ -193,9 +193,8 @@
             weights, jnp.concatenate([values, ones], axis=1), preferred_element_type=F32
         )
 
-    def attend_first(members):
+    def attend_first(members, here=(0, 1, XS - 1)):
         mine = gathered(members)
-        here = (0, 1, XS - 1)
         scores = [score(mine, i) for i in here]
         raw = lax.dot_general(mine, new_keys, contract, preferred_element_type=F32)
         seen = [
@@ -212,6 +211,9 @@
         for i, s in zip(here, scores):
             total += weigh(s, top, i)
         top = jnp.broadcast_to(top, (top.shape[0], HEAD_DIM))
+        if len(here) == XS:
+            finish(members, top, total)
+            return
         for j, d in enumerate(members):
             tops[at_slot[d]] = top[j * block:(j + 1) * block]
             totals[at_slot[d]] = total[j * block:(j + 1) * block]
@@ -224,6 +226,9 @@
         fade = jnp.exp2(before - top)
         total = total * jnp.concatenate([fade, fade], axis=1)
         total += weigh(scores, top[:, :1], 2)
+        finish(members, top, total)
+
+    def finish(members, top, total):
         amount = total[:, HEAD_DIM:]
         full = jnp.maximum(amount, 1.0)
         normal = (total[:, :HEAD_DIM] / full).astype(BF16)
@@ -236,15 +241,13 @@
 
     arrived(kv_all.at[1, :, 1], kv_recv.at[1, 1])
     arrived(kv_all.at[XS - 1, :, 0], kv_recv.at[XS - 1, 0])
-    for t in NEAR:
-        queries_arrived(t)
-    attend_first(FIRST[0])
-    attend_first(FIRST[1])
     queries_arrived(HALF)
     for t in NEAR:
         queries_arrived(SETS[t][1], 2)
     attend_first(FIRST[2])
     attend_first(FIRST[3])
+    for t in NEAR:
+        queries_arrived(t)
     for slot in range(SLOTS):
         arrived(kv_all.at[2, :, slot], kv_recv.at[2, slot])
 
@@ -277,8 +280,8 @@
     attend_second(SECOND[1])
     send_pair(1)
     send_pair(-1)
-    attend_second(SECOND[2])
-    attend_second(SECOND[3])
+    attend_first(FIRST[1], range(XS))
+    attend_first(FIRST[0], range(XS))
     for t in NEAR:
         send_near(t)
 

time: 43.9 us -> 43.3 us (0.986)
  Pallas kernels: 43.2 us -> 42.5 us
    pallas_call x1, Pallas kernels: 43.2 us -> 42.5 us  [local(): pl.pallas_call(functools.partial(kernel, hs, rows, group), out_shape=jax....]
where the time goes in v5:
time: 43.3 us; the launch traced here: 43.1 us
  Pallas kernels  42.5 us (98%)
  local copies, waits for them, and re-layouts  0.62 us (1%)
    pallas_call x1, Pallas kernels, local(): pl.pallas_call(functools.partial(kernel, hs, rows, group), out_shape=jax....  42.5 us

profile of v5, /device:TPU:1, one launch (start us, length us, event | category | flops | bytes accessed | tf_op | source)
XLA Modules:
  0.0 43.1 jit_solution(295155947070439241)
XLA Ops:
  0.0 42.5 %shard_map.55 = bf16[1,8192]{1,0:T(2,128)(2,1)S(1)} custom-call(s32[2]{0:T(128)} %lens_hbm.1, s32[2,64]{1,0:T(2,128)} %slot_hbm.1, bf16[8,1024]{1,0:T(8,128)(2,1)} %q_hbm.1, bf16[2,8,128]{2,1,0:T(8,128)(2,1)} %new_hbm.1, bf16[2,2,256,128]{3,2,1,0:T(8,128)(2,1)} %cache_hbm.1), custom_call_target="tpu_custom_call" | custom-call | tf_op jit(solution)/shard_map/pallas_call | solution.py:354
  42.5 0.6 %copy.7 = bf16[1,8192]{1,0:T(2,128)(2,1)} copy(bf16[1,8192]{1,0:T(2,128)(2,1)S(1)} %shard_map.55) | data formatting | bytes 32768

commit v6 on v5

--- a/solution.py
+++ b/solution.py
@@ -27,7 +27,7 @@
 ORDER = sum(SETS.values(), ()) + (-FAR, FAR, 0, HALF)
 FIRST = (NEAR, (0, -FAR, FAR), (-3, 7, -7, 3, HALF), (-4, 6, -6, 4))
 SECOND = (FIRST[2], FIRST[3], FIRST[1], FIRST[0])
-PARTNERS = (1, -1, 2, -2, RELAY, -RELAY, FAR, -FAR)
+PARTNERS = (FAR, -FAR, RELAY, -RELAY, 2, -2, 1, -1)
 
 
 def merge(diagonal, terms):
@@ -310,7 +310,7 @@
         merged, stat = merge(diagonal, terms)
         final[1 + number] = merged.astype(BF16).reshape(rows, group, HEAD_DIM)
         final_stat[1 + number] = stat
-        for k in range(hs):
+        for k in sorted(range(hs), key=lambda k: -min(k, hs - k)):
             send_final(1 + number, d, k)
     terms = [(part[at_slot[0]], part_stat[at_slot[0]])]
     for i in range(len(NEAR)):

time: 43.3 us -> 42.9 us (level)
  no operation moved by 1% of the time
where the time goes in v6:
time: 42.9 us; the launch traced here: 42.7 us
  Pallas kernels  42.1 us (98%)
  local copies, waits for them, and re-layouts  0.62 us (1%)
    pallas_call x1, Pallas kernels, local(): pl.pallas_call(functools.partial(kernel, hs, rows, group), out_shape=jax....  42.1 us

profile of v6, /device:TPU:1, one launch (start us, length us, event | category | flops | bytes accessed | tf_op | source)
XLA Modules:
  0.0 42.7 jit_solution(10377291452862021345)
XLA Ops:
  0.0 42.1 %shard_map.55 = bf16[1,8192]{1,0:T(2,128)(2,1)S(1)} custom-call(s32[2]{0:T(128)} %lens_hbm.1, s32[2,64]{1,0:T(2,128)} %slot_hbm.1, bf16[8,1024]{1,0:T(8,128)(2,1)} %q_hbm.1, bf16[2,8,128]{2,1,0:T(8,128)(2,1)} %new_hbm.1, bf16[2,2,256,128]{3,2,1,0:T(8,128)(2,1)} %cache_hbm.1), custom_call_target="tpu_custom_call" | custom-call | tf_op jit(solution)/shard_map/pallas_call | solution.py:354
  42.1 0.6 %copy.7 = bf16[1,8192]{1,0:T(2,128)(2,1)} copy(bf16[1,8192]{1,0:T(2,128)(2,1)S(1)} %shard_map.55) | data formatting | bytes 32768
